TPU v7x, 256 devices: a whole 4x4x8 slice. The times are simulated.
256 devices in a mesh: ctx: 64 (over z, x, y_hi), ch: 4 (over y_lo, core).
Axes of the slice: x: 4, y: 4 (y_hi: 2, y_lo: 2; y = y_hi * 2 + y_lo), z: 8, core: 2. Of those that a mesh axis runs over, the one named last changes fastest.
Arguments:
- query: bfloat16 [8192, 8192], P('ctx', 'ch'), may hold values from -6 to 6
- key: bfloat16 [8192, 8192], P('ctx', 'ch'), may hold values from -6 to 6
- value: bfloat16 [8192, 8192], P('ctx', 'ch'), may hold values from -6 to 6
- filter_taps: bfloat16 [1024, 512], P('ctx', 'ch'), may hold values from -0.1875 to 0.1875
- skip: float32 [8192], P('ch'), may hold values from -1 to 1
Outputs:
- gated: bfloat16 [8192, 8192], P('ctx', 'ch')
All inputs are finite; a program needn't handle non-finite values.
Results may differ from a plain program's by a relative error of at most 0.0085.
Values may be sent and summed in bfloat16 or wider, within the bound.
A program may use at most 192 MiB of HBM per device.

v0:
```python
import jax
import jax.numpy as jnp
from jax import lax
from jax.sharding import PartitionSpec as P

GROUP = 16
BLOCK = 128
LAGS = 8


def from_behind(value, axis, steps):
    count = lax.axis_size(axis)
    leading, last = (max(0, -steps), min(count, count - steps))
    return lax.ppermute(value, axis, [(source, source + steps) for source in range(leading, last)])


def all_toeplitz(padded, width, count):
    lag_part = jnp.arange(count, dtype=jnp.int32)[:, None, None] * width
    row_part = jnp.arange(width, dtype=jnp.int32)[None, :, None]
    col_part = jnp.arange(width, dtype=jnp.int32)[None, None, :]
    indices = lag_part + width + row_part - col_part
    return jnp.take(padded, indices, axis=1)


def per_device(query, key, value, filter_taps, skip):
    rows = query.shape[0]
    channels = query.shape[1]
    groups = channels // GROUP
    all_taps = lax.all_gather(filter_taps, "ctx", axis=0, tiled=True)
    mixed = (key.astype(jnp.float32) * value.astype(jnp.float32)).astype(jnp.bfloat16)
    mixed_cols = mixed.T.reshape(groups, GROUP, rows)
    padded = jnp.concatenate(
        [
            jnp.zeros((groups, BLOCK), jnp.bfloat16),
            all_taps.T,
            jnp.zeros((groups, BLOCK), jnp.bfloat16),
        ],
        axis=1,
    )
    toeplitz_all = all_toeplitz(padded, BLOCK, LAGS)

    def convolve(lag_index, source):
        return jnp.einsum(
            "gts,gcs->gct", toeplitz_all[:, lag_index], source, preferred_element_type=jnp.float32
        )

    summed = convolve(0, mixed_cols)
    moving = mixed_cols
    for lag_index in range(1, LAGS):
        moving = from_behind(moving, "ctx", 1)
        summed = summed + convolve(lag_index, moving)
    conv = summed.reshape(channels, rows).T
    gated = query.astype(jnp.float32) * (conv + skip[None, :] * mixed.astype(jnp.float32))
    return gated.astype(jnp.bfloat16)


def solution(mesh):
    placed = (P("ctx", "ch"), P("ctx", "ch"), P("ctx", "ch"), P("ctx", "ch"), P("ch"))
    return jax.shard_map(
        per_device, mesh=mesh, in_specs=placed, out_specs=P("ctx", "ch"), check_vma=False
    )
```

profile of v0, /device:TPU:128, one launch (start us, length us, event | category | flops | bytes accessed | tf_op | source)
XLA Modules:
  0.0 821.1 jit_solution(8726122279715097564)
XLA Ops:
  0.0 1.3 fusion.20
  1.3 0.3 copy.8
  1.6 5.1 collective-permute-start
  6.7 0.1 iota_add_fusion
  6.8 0.2 compare_select_fusion
  7.0 15.9 %collective-permute-done = bf16[128,16,128]{2,1,0:T(8,128)(2,1)S(1)} collective-permute-done((bf16[128,16,128]{2,1,0:T(8,128)(2,1)S(1)}, bf16[128,16,128]{2,1,0:T(8,128)(2,1)S(1)}, u32[]{:S(2)}, u32[]{:S(2)}) %collective-permute-start) | collective-permute-done | bytes 524320 | tf_op jit(solution)/shard_map/ppermute | solution.py:14
  22.9 1.9 collective-permute-start.1
  24.8 0.1 broadcast_clamp_fusion
  24.9 18.4 %collective-permute-done.1 = bf16[128,16,128]{2,1,0:T(8,128)(2,1)S(1)} collective-permute-done((bf16[128,16,128]{2,1,0:T(8,128)(2,1)S(1)}, bf16[128,16,128]{2,1,0:T(8,128)(2,1)S(1)}, u32[]{:S(2)}, u32[]{:S(2)}) %collective-permute-start.1) | collective-permute-done | bytes 524320 | tf_op jit(solution)/shard_map/ppermute | solution.py:14
  43.3 1.9 collective-permute-start.2
  45.2 183.3 %all_gather.3 = bf16[1024,128]{1,0:T(8,128)(2,1)S(1)} all-gather(bf16[16,128]{1,0:T(8,128)(2,1)} %param.8), channel_id=1, replica_groups=mesh['ctx'=64,'ch'=4] {'ctx'}, dimensions={0}, use_global_device_ids=true | all-gather | bytes 266240 | tf_op jit(solution)/shard_map/all_gather | solution.py:29
  228.5 453.9 %gather_fusion = bf16[131072,128]{1,0:T(8,128)(2,1)} fusion(bf16[128,1280]{0,1:T(8,128)(2,1)S(1)} %pad_maximum_fusion, s32[131072]{0:T(1024)S(1)} %broadcast_clamp_fusion), kind=kCustom, calls=%fused_computation | custom fusion | bytes 67633152 | tf_op jit(solution)/shard_map/jit(_take)/gather | solution.py:22
  682.4 46.0 %copy.9 = bf16[8,128,128,128]{2,1,3,0:T(8,128)(2,1)} copy(bf16[8,128,128,128]{3,2,1,0:T(8,128)(2,1)} %bitcast.61) | data formatting | bytes 67108864 | tf_op jit(solution)/shard_map/jit(_take)/gather | solution.py:22
  728.4 0.2 fusion.19
  728.7 5.4 collective-permute-start.3
  734.1 23.2 %select_bitcast_fusion = bf16[128,8,128,128]{3,2,0,1:T(8,128)(2,1)} fusion(bf16[8,128,128,128]{2,1,3,0:T(8,128)(2,1)} %copy.9, pred[8,128,128]{2,1,0:T(8,128)(4,1)S(1)} %fusion.19), kind=kLoop, calls=%fused_computation.1 | loop fusion | flops 16777216 | bytes 67239936 | tf_op jit(solution)/shard_map/jit(_take)/select_n | solution.py:22
  757.3 4.5 fusion.7
  761.8 1.9 collective-permute-start.4
  763.8 4.5 fusion.8
  768.3 4.5 fusion.9
  772.7 7.8 collective-permute-done.4
  780.6 1.9 collective-permute-start.5
  782.5 4.6 fusion.10
  787.1 4.7 fusion.11
  791.8 5.6 collective-permute-done.5
  797.4 1.9 collective-permute-start.6
  799.3 4.5 fusion.12
  803.7 4.5 fusion.13
  808.2 5.9 collective-permute-done.6
  814.1 4.5 fusion.14
  818.6 0.4 copy.10
  819.0 2.1 fusion.16
  (15 shorter events, 0.1 us)
Async XLA Ops:
  1.6 21.3 %collective-permute-start = (bf16[128,16,128]{2,1,0:T(8,128)(2,1)S(1)}, bf16[128,16,128]{2,1,0:T(8,128)(2,1)S(1)}, u32[]{:S(2)}, u32[]{:S(2)}) collective-permute-start(bf16[128,16,128]{2,1,0:T(8,128)(2,1)S(1)} %bitcast.64), channel_id=1, source_target_pairs={{0,4},{4,8},{8,12},{12,16},{16,20},{20,24},{24,28},{28,32},{32,36}... | collective-permute-start | bytes 1572872 | tf_op jit(solution)/shard_map/ppermute | solution.py:14
  22.9 20.4 %collective-permute-start.1 = (bf16[128,16,128]{2,1,0:T(8,128)(2,1)S(1)}, bf16[128,16,128]{2,1,0:T(8,128)(2,1)S(1)}, u32[]{:S(2)}, u32[]{:S(2)}) collective-permute-start(bf16[128,16,128]{2,1,0:T(8,128)(2,1)S(1)} %collective-permute-done), channel_id=1, source_target_pairs={{0,4},{4,8},{8,12},{12,16},{16,20},{20,24},{24,28},{28,32},{32,36}... | collective-permute-start | bytes 1572872 | tf_op jit(solution)/shard_map/ppermute | solution.py:14
  43.3 639.1 %copy-start.2 = (bf16[128,16,128]{2,1,0:T(8,128)(2,1)}, bf16[128,16,128]{2,1,0:T(8,128)(2,1)S(1)}, u32[]{:S(2)}) copy-start(bf16[128,16,128]{2,1,0:T(8,128)(2,1)S(1)} %collective-permute-done.1) | copy-start | bytes 1572868
  43.3 685.4 %collective-permute-start.2 = (bf16[128,16,128]{2,1,0:T(8,128)(2,1)S(1)}, bf16[128,16,128]{2,1,0:T(8,128)(2,1)}, u32[]{:S(2)}, u32[]{:S(2)}) collective-permute-start(bf16[128,16,128]{2,1,0:T(8,128)(2,1)S(1)} %collective-permute-done.1), channel_id=1, source_target_pairs={{0,4},{4,8},{8,12},{12,16},{16,20},{20,24},{24,28},{28,32},{32,36}... | collective-permute-start | bytes 1572872 | tf_op jit(solution)/shard_map/ppermute | solution.py:14
  728.7 39.6 %copy-start.3 = (bf16[128,16,128]{2,1,0:T(8,128)(2,1)S(1)}, bf16[128,16,128]{2,1,0:T(8,128)(2,1)}, u32[]{:S(2)}) copy-start(bf16[128,16,128]{2,1,0:T(8,128)(2,1)} %copy-done.2) | copy-start | bytes 1572868
  728.7 33.2 %collective-permute-start.3 = (bf16[128,16,128]{2,1,0:T(8,128)(2,1)}, bf16[128,16,128]{2,1,0:T(8,128)(2,1)}, u32[]{:S(2)}, u32[]{:S(2)}) collective-permute-start(bf16[128,16,128]{2,1,0:T(8,128)(2,1)} %collective-permute-done.2), channel_id=1, source_target_pairs={{0,4},{4,8},{8,12},{12,16},{16,20},{20,24},{24,28},{28,32},{32,36}... | collective-permute-start | bytes 1572872 | tf_op jit(solution)/shard_map/ppermute | solution.py:14
  757.3 61.7 %copy-start = (bf16[128,2048]{1,0:T(8,128)(2,1)S(1)}, bf16[128,2048]{1,0:T(8,128)(2,1)}, u32[]{:S(2)}) copy-start(bf16[128,2048]{1,0:T(8,128)(2,1)} %param.7) | copy-start | bytes 1572868
  757.3 61.7 %copy-start.1 = (bf16[128,2048]{1,0:T(8,128)(2,1)S(1)}, bf16[128,2048]{1,0:T(8,128)(2,1)}, u32[]{:S(2)}) copy-start(bf16[128,2048]{1,0:T(8,128)(2,1)} %param.6) | copy-start | bytes 1572868
  757.3 61.7 %copy-start.4 = (f32[2048]{0:T(1024)S(1)}, f32[2048]{0:T(1024)}, u32[]{:S(2)}) copy-start(f32[2048]{0:T(1024)} %param.9) | copy-start | bytes 24580
  761.8 18.7 %collective-permute-start.4 = (bf16[128,16,128]{2,1,0:T(8,128)(2,1)}, bf16[128,16,128]{2,1,0:T(8,128)(2,1)S(1)}, u32[]{:S(2)}, u32[]{:S(2)}) collective-permute-start(bf16[128,16,128]{2,1,0:T(8,128)(2,1)} %collective-permute-done.3), channel_id=1, source_target_pairs={{0,4},{4,8},{8,12},{12,16},{16,20},{20,24},{24,28},{28,32},{32,36}... | collective-permute-start | bytes 1572872 | tf_op jit(solution)/shard_map/ppermute | solution.py:14
  780.6 16.8 %collective-permute-start.5 = (bf16[128,16,128]{2,1,0:T(8,128)(2,1)S(1)}, bf16[128,16,128]{2,1,0:T(8,128)(2,1)S(1)}, u32[]{:S(2)}, u32[]{:S(2)}) collective-permute-start(bf16[128,16,128]{2,1,0:T(8,128)(2,1)S(1)} %collective-permute-done.4), channel_id=1, source_target_pairs={{0,4},{4,8},{8,12},{12,16},{16,20},{20,24},{24,28},{28,32},{32,36}... | collective-permute-start | bytes 1572872 | tf_op jit(solution)/shard_map/ppermute | solution.py:14
  797.4 16.8 %collective-permute-start.6 = (bf16[128,16,128]{2,1,0:T(8,128)(2,1)S(1)}, bf16[128,16,128]{2,1,0:T(8,128)(2,1)S(1)}, u32[]{:S(2)}, u32[]{:S(2)}) collective-permute-start(bf16[128,16,128]{2,1,0:T(8,128)(2,1)S(1)} %collective-permute-done.5), channel_id=1, source_target_pairs={{0,4},{4,8},{8,12},{12,16},{16,20},{20,24},{24,28},{28,32},{32,36}... | collective-permute-start | bytes 1572872 | tf_op jit(solution)/shard_map/ppermute | solution.py:14
where the time goes:
time: 823 us; the launch traced here: 821 us
  local copies, waits for them, and re-layouts  501 us (61%)
  blocking collectives  183 us (22%)
  waiting for transfers between devices  53.6 us (7%)
  matrix products  36.2 us (4%)
  other arithmetic  27.2 us (3%)
  starting transfers between devices  20.1 us (2%)
    gather x2, local copies, waits for them, and re-layouts, all_toeplitz(): return jnp.take(padded, indices, axis=1)  500 us
    all_gather x1, blocking collectives, per_device(): all_taps = lax.all_gather(filter_taps, 'ctx', axis=0, tiled=True)  183 us
    ppermute x7, waiting for transfers between devices, from_behind(): lax.ppermute(value, axis, [(source, source + steps) for source in range(l...  53.6 us
    dot_general x8, matrix products, convolve(): jnp.einsum('gts,gcs->gct', toeplitz_all[:, lag_index], source, preferred_...  36.2 us
    select_n x2, other arithmetic, all_toeplitz(): return jnp.take(padded, indices, axis=1)  23.4 us
    ppermute x7, starting transfers between devices, from_behind(): lax.ppermute(value, axis, [(source, source + steps) for source in range(l...  20.1 us
  transfers between devices with their start and end apart: 7, of which 5 were waited for; matrix products, arithmetic and copies ran while one was open for 68% of the time, Pallas kernels for 0%

commit v1 on v0

--- a/solution.py
+++ b/solution.py
@@ -26,7 +26,10 @@
     rows = query.shape[0]
     channels = query.shape[1]
     groups = channels // GROUP
-    all_taps = lax.all_gather(filter_taps, "ctx", axis=0, tiled=True)
+    size = lax.axis_size("ctx")
+    shards = jnp.stack([filter_taps for _ in range(size)])
+    shards = lax.all_to_all(shards, "ctx", split_axis=0, concat_axis=0)
+    all_taps = jnp.concatenate(shards, axis=0)
     mixed = (key.astype(jnp.float32) * value.astype(jnp.float32)).astype(jnp.bfloat16)
     mixed_cols = mixed.T.reshape(groups, GROUP, rows)
     padded = jnp.concatenate(

time: 823 us -> 642 us (0.78)
  blocking collectives: 183 us -> 0 us
  waiting for transfers between devices: 53.6 us -> 43.9 us
    all_gather x1 -> x0, blocking collectives: 183 us -> none  [per_device(): all_taps = lax.all_gather(filter_taps, 'ctx', axis=0, tiled=True)]
    all_to_all x0 -> x1, starting transfers between devices: none -> 10.7 us  [per_device(): shards = lax.all_to_all(shards, 'ctx', split_axis=0, concat_axis=0)]
    ppermute x7, waiting for transfers between devices: 53.6 us -> 43.9 us  [from_behind(): lax.ppermute(value, axis, [(source, source + steps) for source in range(l...]
  transfers between devices with their start and end apart: 7 -> 8, of which waited for: 5 -> 5; matrix products, arithmetic and copies ran while one was open for 68% -> 87% of each run, Pallas kernels for 0% -> 0%
where the time goes in v1:
time: 642 us; the launch traced here: 640 us
  local copies, waits for them, and re-layouts  505 us (79%)
  waiting for transfers between devices  43.9 us (7%)
  matrix products  36.3 us (6%)
  starting transfers between devices  27.5 us (4%)
  other arithmetic  27.2 us (4%)
    gather x2, local copies, waits for them, and re-layouts, all_toeplitz(): return jnp.take(padded, indices, axis=1)  503 us
    ppermute x7, waiting for transfers between devices, from_behind(): lax.ppermute(value, axis, [(source, source + steps) for source in range(l...  43.9 us
    dot_general x8, matrix products, convolve(): jnp.einsum('gts,gcs->gct', toeplitz_all[:, lag_index], source, preferred_...  36.3 us
    select_n x2, other arithmetic, all_toeplitz(): return jnp.take(padded, indices, axis=1)  23.4 us
    ppermute x7, starting transfers between devices, from_behind(): lax.ppermute(value, axis, [(source, source + steps) for source in range(l...  16.7 us
  transfers between devices with their start and end apart: 8, of which 5 were waited for; matrix products, arithmetic and copies ran while one was open for 87% of the time, Pallas kernels for 0%

profile of v1, /device:TPU:128, one launch (start us, length us, event | category | flops | bytes accessed | tf_op | source)
XLA Modules:
  0.0 640.2 jit_solution(329885496168630649)
XLA Ops:
  0.0 1.3 fusion.20
  1.3 0.3 copy.8
  1.6 5.1 collective-permute-start
  6.7 1.4 stack.2
  8.1 10.7 %all-to-all-start = ((bf16[64,16,128]{2,1,0:T(8,128)(2,1)}), bf16[64,16,128]{2,1,0:T(8,128)(2,1)S(1)}, u32[]{:S(2)}, u32[]{:S(2)}) async-start(bf16[64,16,128]{2,1,0:T(8,128)(2,1)} %stack.2), calls=%async_computation | async-start | bytes 524288 | tf_op jit(solution)/shard_map/all_to_all | solution.py:31
  18.9 4.4 collective-permute-done
  23.2 1.9 collective-permute-start.1
  25.2 0.1 iota_add_fusion
  25.2 0.2 compare_select_fusion
  25.5 17.8 %collective-permute-done.1 = bf16[128,16,128]{2,1,0:T(8,128)(2,1)S(1)} collective-permute-done((bf16[128,16,128]{2,1,0:T(8,128)(2,1)S(1)}, bf16[128,16,128]{2,1,0:T(8,128)(2,1)S(1)}, u32[]{:S(2)}, u32[]{:S(2)}) %collective-permute-start.1) | collective-permute-done | bytes 524320 | tf_op jit(solution)/shard_map/ppermute | solution.py:14
  43.3 1.9 collective-permute-start.2
  45.3 0.2 fusion.19
  45.6 457.1 %gather_fusion = bf16[131072,128]{1,0:T(8,128)(2,1)} fusion(bf16[128,1280]{0,1:T(8,128)(2,1)S(1)} %pad_maximum_fusion, s32[131072]{0:T(1024)S(1)} %broadcast_clamp_fusion), kind=kCustom, calls=%fused_computation | custom fusion | bytes 67633152 | tf_op jit(solution)/shard_map/jit(_take)/gather | solution.py:22
  502.7 45.9 %copy.9 = bf16[8,128,128,128]{2,1,3,0:T(8,128)(2,1)} copy(bf16[8,128,128,128]{3,2,1,0:T(8,128)(2,1)} %bitcast.63) | data formatting | bytes 67108864 | tf_op jit(solution)/shard_map/jit(_take)/gather | solution.py:22
  548.6 2.0 collective-permute-start.3
  550.6 23.2 %select_bitcast_fusion = bf16[128,8,128,128]{3,2,0,1:T(8,128)(2,1)} fusion(bf16[8,128,128,128]{2,1,3,0:T(8,128)(2,1)} %copy.9, pred[8,128,128]{2,1,0:T(8,128)(4,1)S(1)} %fusion.19), kind=kLoop, calls=%fused_computation.1 | loop fusion | flops 16777216 | bytes 67239936 | tf_op jit(solution)/shard_map/jit(_take)/select_n | solution.py:22
  573.8 4.5 fusion.7
  578.3 1.9 collective-permute-start.4
  580.3 4.5 fusion.8
  584.8 4.7 fusion.9
  589.4 8.3 %collective-permute-done.4 = bf16[128,16,128]{2,1,0:T(8,128)(2,1)S(1)} collective-permute-done((bf16[128,16,128]{2,1,0:T(8,128)(2,1)}, bf16[128,16,128]{2,1,0:T(8,128)(2,1)S(1)}, u32[]{:S(2)}, u32[]{:S(2)}) %collective-permute-start.4) | collective-permute-done | bytes 524320 | tf_op jit(solution)/shard_map/ppermute | solution.py:14
  597.7 1.9 collective-permute-start.5
  599.6 4.6 fusion.10
  604.3 4.7 fusion.11
  608.9 7.0 %collective-permute-done.5 = bf16[128,16,128]{2,1,0:T(8,128)(2,1)S(1)} collective-permute-done((bf16[128,16,128]{2,1,0:T(8,128)(2,1)S(1)}, bf16[128,16,128]{2,1,0:T(8,128)(2,1)S(1)}, u32[]{:S(2)}, u32[]{:S(2)}) %collective-permute-start.5) | collective-permute-done | bytes 524320 | tf_op jit(solution)/shard_map/ppermute | solution.py:14
  615.9 1.9 collective-permute-start.6
  617.8 4.5 fusion.12
  622.3 4.5 fusion.13
  626.8 6.4 %collective-permute-done.6 = bf16[128,16,128]{2,1,0:T(8,128)(2,1)S(1)} collective-permute-done((bf16[128,16,128]{2,1,0:T(8,128)(2,1)S(1)}, bf16[128,16,128]{2,1,0:T(8,128)(2,1)S(1)}, u32[]{:S(2)}, u32[]{:S(2)}) %collective-permute-start.6) | collective-permute-done | bytes 524320 | tf_op jit(solution)/shard_map/ppermute | solution.py:14
  633.2 4.5 fusion.14
  637.7 0.4 copy.10
  638.0 2.1 fusion.16
  (19 shorter events, 0.1 us)
Async XLA Ops:
  1.6 21.6 %collective-permute-start = (bf16[128,16,128]{2,1,0:T(8,128)(2,1)S(1)}, bf16[128,16,128]{2,1,0:T(8,128)(2,1)S(1)}, u32[]{:S(2)}, u32[]{:S(2)}) collective-permute-start(bf16[128,16,128]{2,1,0:T(8,128)(2,1)S(1)} %bitcast.66), channel_id=1, source_target_pairs={{0,4},{4,8},{8,12},{12,16},{16,20},{20,24},{24,28},{28,32},{32,36}... | collective-permute-start | bytes 1572872 | tf_op jit(solution)/shard_map/ppermute | solution.py:14
  8.1 37.4 %all-to-all-start = ((bf16[64,16,128]{2,1,0:T(8,128)(2,1)}), bf16[64,16,128]{2,1,0:T(8,128)(2,1)S(1)}, u32[]{:S(2)}, u32[]{:S(2)}) async-start(bf16[64,16,128]{2,1,0:T(8,128)(2,1)} %stack.2), calls=%async_computation | async-start | bytes 524288 | tf_op jit(solution)/shard_map/all_to_all | solution.py:31
  23.2 22.0 %copy-start.2 = (bf16[128,16,128]{2,1,0:T(8,128)(2,1)}, bf16[128,16,128]{2,1,0:T(8,128)(2,1)S(1)}, u32[]{:S(2)}) copy-start(bf16[128,16,128]{2,1,0:T(8,128)(2,1)S(1)} %collective-permute-done) | copy-start | bytes 1572868
  23.2 20.0 %collective-permute-start.1 = (bf16[128,16,128]{2,1,0:T(8,128)(2,1)S(1)}, bf16[128,16,128]{2,1,0:T(8,128)(2,1)S(1)}, u32[]{:S(2)}, u32[]{:S(2)}) collective-permute-start(bf16[128,16,128]{2,1,0:T(8,128)(2,1)S(1)} %collective-permute-done), channel_id=1, source_target_pairs={{0,4},{4,8},{8,12},{12,16},{16,20},{20,24},{24,28},{28,32},{32,36}... | collective-permute-start | bytes 1572872 | tf_op jit(solution)/shard_map/ppermute | solution.py:14
  43.3 459.4 %copy-start.4 = (bf16[128,16,128]{2,1,0:T(8,128)(2,1)}, bf16[128,16,128]{2,1,0:T(8,128)(2,1)S(1)}, u32[]{:S(2)}) copy-start(bf16[128,16,128]{2,1,0:T(8,128)(2,1)S(1)} %collective-permute-done.1) | copy-start | bytes 1572868
  43.3 505.3 %collective-permute-start.2 = (bf16[128,16,128]{2,1,0:T(8,128)(2,1)S(1)}, bf16[128,16,128]{2,1,0:T(8,128)(2,1)}, u32[]{:S(2)}, u32[]{:S(2)}) collective-permute-start(bf16[128,16,128]{2,1,0:T(8,128)(2,1)S(1)} %collective-permute-done.1), channel_id=1, source_target_pairs={{0,4},{4,8},{8,12},{12,16},{16,20},{20,24},{24,28},{28,32},{32,36}... | collective-permute-start | bytes 1572872 | tf_op jit(solution)/shard_map/ppermute | solution.py:14
  548.5 31.7 %copy-start.3 = (bf16[128,16,128]{2,1,0:T(8,128)(2,1)S(1)}, bf16[128,16,128]{2,1,0:T(8,128)(2,1)}, u32[]{:S(2)}) copy-start(bf16[128,16,128]{2,1,0:T(8,128)(2,1)} %copy-done.2) | copy-start | bytes 1572868
  548.6 29.8 %collective-permute-start.3 = (bf16[128,16,128]{2,1,0:T(8,128)(2,1)}, bf16[128,16,128]{2,1,0:T(8,128)(2,1)}, u32[]{:S(2)}, u32[]{:S(2)}) collective-permute-start(bf16[128,16,128]{2,1,0:T(8,128)(2,1)} %collective-permute-done.2), channel_id=1, source_target_pairs={{0,4},{4,8},{8,12},{12,16},{16,20},{20,24},{24,28},{28,32},{32,36}... | collective-permute-start | bytes 1572872 | tf_op jit(solution)/shard_map/ppermute | solution.py:14
  573.8 64.2 %copy-start = (bf16[128,2048]{1,0:T(8,128)(2,1)S(1)}, bf16[128,2048]{1,0:T(8,128)(2,1)}, u32[]{:S(2)}) copy-start(bf16[128,2048]{1,0:T(8,128)(2,1)} %param.7) | copy-start | bytes 1572868
  573.8 64.2 %copy-start.1 = (bf16[128,2048]{1,0:T(8,128)(2,1)S(1)}, bf16[128,2048]{1,0:T(8,128)(2,1)}, u32[]{:S(2)}) copy-start(bf16[128,2048]{1,0:T(8,128)(2,1)} %param.6) | copy-start | bytes 1572868
  573.8 64.3 %copy-start.5 = (f32[2048]{0:T(1024)S(1)}, f32[2048]{0:T(1024)}, u32[]{:S(2)}) copy-start(f32[2048]{0:T(1024)} %param.9) | copy-start | bytes 24580
  578.3 19.4 %collective-permute-start.4 = (bf16[128,16,128]{2,1,0:T(8,128)(2,1)}, bf16[128,16,128]{2,1,0:T(8,128)(2,1)S(1)}, u32[]{:S(2)}, u32[]{:S(2)}) collective-permute-start(bf16[128,16,128]{2,1,0:T(8,128)(2,1)} %collective-permute-done.3), channel_id=1, source_target_pairs={{0,4},{4,8},{8,12},{12,16},{16,20},{20,24},{24,28},{28,32},{32,36}... | collective-permute-start | bytes 1572872 | tf_op jit(solution)/shard_map/ppermute | solution.py:14
  597.7 18.2 %collective-permute-start.5 = (bf16[128,16,128]{2,1,0:T(8,128)(2,1)S(1)}, bf16[128,16,128]{2,1,0:T(8,128)(2,1)S(1)}, u32[]{:S(2)}, u32[]{:S(2)}) collective-permute-start(bf16[128,16,128]{2,1,0:T(8,128)(2,1)S(1)} %collective-permute-done.4), channel_id=1, source_target_pairs={{0,4},{4,8},{8,12},{12,16},{16,20},{20,24},{24,28},{28,32},{32,36}... | collective-permute-start | bytes 1572872 | tf_op jit(solution)/shard_map/ppermute | solution.py:14
  615.9 17.3 %collective-permute-start.6 = (bf16[128,16,128]{2,1,0:T(8,128)(2,1)S(1)}, bf16[128,16,128]{2,1,0:T(8,128)(2,1)S(1)}, u32[]{:S(2)}, u32[]{:S(2)}) collective-permute-start(bf16[128,16,128]{2,1,0:T(8,128)(2,1)S(1)} %collective-permute-done.5), channel_id=1, source_target_pairs={{0,4},{4,8},{8,12},{12,16},{16,20},{20,24},{24,28},{28,32},{32,36}... | collective-permute-start | bytes 1572872 | tf_op jit(solution)/shard_map/ppermute | solution.py:14
